TPU v7x, 512 devices: a whole 4x8x8 slice. The times are simulated.
512 devices in a mesh: wide: 8 (over y), row: 64 (over z, x, core).
Axes of the slice: x: 4, y: 8, z: 8, core: 2. Of those that a mesh axis runs over, the one named last changes fastest.
Arguments:
- columns: float32 [16384, 2048], P('row', 'wide'), may hold values from -40 to 40, as said below
Outputs:
- rotated: float32 [16384, 2048], P('row', 'wide')
Inputs may be any that keep to these rules, and one draw needn't show every extreme that they name: `columns`: columns have differing scales.
All inputs are finite; a program needn't handle non-finite values.
Results may differ from a plain program's by a relative error of at most 0.00021.
Values sent between devices are 32-bit elements; how exact they have to be, the bound alone decides.
A program may use at most 64 MiB of HBM per device.

v0:
```python
import jax
import jax.numpy as jnp
from jax import lax
from jax.sharding import PartitionSpec as P

ROUNDS = 4


def passed_along(x, axis, by):
    length = lax.axis_size(axis)
    return lax.ppermute(x, axis, [(i, (i + by) % length) for i in range(length)])


def rotation(gram_matrix):
    width_count = gram_matrix.shape[0]
    positions = jnp.arange(width_count)
    signs = jnp.where(positions[:, None] < positions[None, :], 1.0, -1.0).astype(jnp.float32)
    column_norms = jnp.diagonal(gram_matrix)
    off_diagonal = gram_matrix - jnp.diag(column_norms)
    generator = signs * off_diagonal / (column_norms[:, None] + column_norms[None, :] + 1e-06)
    identity = jnp.eye(width_count, dtype=jnp.float32)
    cayley_half = identity + 0.5 * generator
    normal_matrix = jnp.dot(cayley_half.T, cayley_half, precision=lax.Precision.HIGHEST)
    lower_factor = jnp.linalg.cholesky(normal_matrix)
    partial_solve = lax.linalg.triangular_solve(
        lower_factor, cayley_half, left_side=True, lower=True
    )
    solved = lax.linalg.triangular_solve(
        lower_factor, partial_solve, left_side=True, lower=True, transpose_a=True
    )
    return jnp.dot(cayley_half, solved, precision=lax.Precision.HIGHEST)


def inner_rows(left, right):
    return lax.dot_general(
        left,
        right,
        (((0,), (0,)), ((), ())),
        precision=lax.Precision.HIGHEST,
        preferred_element_type=jnp.float32,
    )


def full_gram(paired):
    return lax.psum(inner_rows(paired, paired), "row")


def per_device(columns):
    block_width = columns.shape[1] // 2
    uppers = columns[:, :block_width]
    lowers = columns[:, block_width:]
    for rounds_done in range(ROUNDS):
        if rounds_done > 0:
            lowers = passed_along(lowers, "wide", 1)
        paired = jnp.concatenate([uppers, lowers], axis=1)
        gram_matrix = full_gram(paired)
        turn = rotation(gram_matrix)
        turned = jnp.dot(paired, turn, precision=lax.Precision.HIGHEST)
        uppers = turned[:, :block_width]
        lowers = turned[:, block_width:]
    lowers = passed_along(lowers, "wide", -(ROUNDS - 1))
    return jnp.concatenate([uppers, lowers], axis=1)


def solution(mesh):
    return jax.shard_map(
        per_device,
        mesh=mesh,
        in_specs=(P("row", "wide"),),
        out_specs=P("row", "wide"),
        check_vma=False,
    )
```

profile of v0, /device:TPU:1, one launch (start us, length us, event | category | flops | bytes accessed | tf_op | source)
XLA Modules:
  0.0 1072.2 jit_solution(15176099788837431226)
XLA Ops:
  8.9 194.4 %all-reduce.6.cloned.1.call-done = f32[256,256]{1,0:T(8,128)} async-done(((f32[256,256]{1,0:T(8,128)}), f32[256,256]{1,0:T(8,128)}) %all-reduce.6.cloned.1.call-update) | async-done | bytes 262160 | tf_op jit(solution)/shard_map/psum | solution.py:45
  206.9 11.7 %cholesky.214 = f32[128,128]{1,0:T(8,128)S(1)} custom-call(f32[128,128]{1,0:T(8,128)S(1)} %cholesky.346), custom_call_target="Cholesky" | custom-call | tf_op jit(solution)/shard_map/jit(cholesky)/cholesky | solution.py:24
  218.6 9.8 custom-call.31
  228.9 11.7 %cholesky.231 = f32[128,128]{1,0:T(8,128)S(1)} custom-call(f32[128,128]{1,0:T(8,128)S(1)} %convolution_subtract_fusion.11), custom_call_target="Cholesky" | custom-call | tf_op jit(solution)/shard_map/jit(cholesky)/cholesky | solution.py:24
  247.4 19.7 %custom-call.33 = f32[2,128,128]{1,2,0:T(8,128)S(1)} custom-call(f32[2,128,128]{2,1,0:T(8,128)S(1)} %get-tuple-element.61), custom_call_target="InvertDiagBlocksLowerTriangular" | custom-call | tf_op jit(solution)/shard_map/triangular_solve/custom-call.4 | solution.py:28
  273.0 4.9 collective-permute-done
  279.1 183.9 %all-reduce.8.cloned.1.call-done = f32[256,256]{1,0:T(8,128)} async-done(((f32[256,256]{1,0:T(8,128)}), f32[256,256]{1,0:T(8,128)}) %all-reduce.8.cloned.1.call-update) | async-done | bytes 262160 | tf_op jit(solution)/shard_map/psum | solution.py:45
  466.6 11.7 %cholesky.248 = f32[128,128]{1,0:T(8,128)S(1)} custom-call(f32[128,128]{1,0:T(8,128)S(1)} %cholesky.349), custom_call_target="Cholesky" | custom-call | tf_op jit(solution)/shard_map/jit(cholesky)/cholesky | solution.py:24
  478.4 9.8 custom-call.34
  488.6 11.7 %cholesky.265 = f32[128,128]{1,0:T(8,128)S(1)} custom-call(f32[128,128]{1,0:T(8,128)S(1)} %convolution_subtract_fusion.10), custom_call_target="Cholesky" | custom-call | tf_op jit(solution)/shard_map/jit(cholesky)/cholesky | solution.py:24
  507.4 19.7 %custom-call.36 = f32[2,128,128]{1,2,0:T(8,128)S(1)} custom-call(f32[2,128,128]{2,1,0:T(8,128)S(1)} %get-tuple-element.63), custom_call_target="InvertDiagBlocksLowerTriangular" | custom-call | tf_op jit(solution)/shard_map/triangular_solve/custom-call.4 | solution.py:28
  539.1 183.8 %all-reduce.10.cloned.1.call-done = f32[256,256]{1,0:T(8,128)} async-done(((f32[256,256]{1,0:T(8,128)}), f32[256,256]{1,0:T(8,128)}) %all-reduce.10.cloned.1.call-update) | async-done | bytes 262160 | tf_op jit(solution)/shard_map/psum | solution.py:45
  726.4 11.7 %cholesky.282 = f32[128,128]{1,0:T(8,128)S(1)} custom-call(f32[128,128]{1,0:T(8,128)S(1)} %cholesky.352), custom_call_target="Cholesky" | custom-call | tf_op jit(solution)/shard_map/jit(cholesky)/cholesky | solution.py:24
  738.2 9.8 custom-call.37
  748.5 11.7 %cholesky.299 = f32[128,128]{1,0:T(8,128)S(1)} custom-call(f32[128,128]{1,0:T(8,128)S(1)} %convolution_subtract_fusion.9), custom_call_target="Cholesky" | custom-call | tf_op jit(solution)/shard_map/jit(cholesky)/cholesky | solution.py:24
  767.5 19.7 %custom-call.39 = f32[2,128,128]{1,2,0:T(8,128)S(1)} custom-call(f32[2,128,128]{2,1,0:T(8,128)S(1)} %get-tuple-element.65), custom_call_target="InvertDiagBlocksLowerTriangular" | custom-call | tf_op jit(solution)/shard_map/triangular_solve/custom-call.4 | solution.py:28
  793.1 4.8 collective-permute-done.2
  799.1 183.9 %all-reduce.12.cloned.1.call-done = f32[256,256]{1,0:T(8,128)} async-done(((f32[256,256]{1,0:T(8,128)}), f32[256,256]{1,0:T(8,128)}) %all-reduce.12.cloned.1.call-update) | async-done | bytes 262160 | tf_op jit(solution)/shard_map/psum | solution.py:45
  986.6 11.7 %cholesky.316 = f32[128,128]{1,0:T(8,128)S(1)} custom-call(f32[128,128]{1,0:T(8,128)S(1)} %cholesky.355), custom_call_target="Cholesky" | custom-call | tf_op jit(solution)/shard_map/jit(cholesky)/cholesky | solution.py:24
  998.4 9.8 custom-call.40
  1008.7 11.9 %cholesky.333 = f32[128,128]{1,0:T(8,128)S(1)} custom-call(f32[128,128]{1,0:T(8,128)S(1)} %convolution_subtract_fusion.8), custom_call_target="Cholesky" | custom-call | tf_op jit(solution)/shard_map/jit(cholesky)/cholesky | solution.py:24
  1027.5 19.7 %custom-call.42 = f32[2,128,128]{1,2,0:T(8,128)S(1)} custom-call(f32[2,128,128]{2,1,0:T(8,128)S(1)} %get-tuple-element.67), custom_call_target="InvertDiagBlocksLowerTriangular" | custom-call | tf_op jit(solution)/shard_map/triangular_solve/custom-call.4 | solution.py:28
  1049.9 6.2 collective-permute-start.3
  1056.1 8.5 collective-permute-done.3
  (154 shorter events, 86.8 us)
Async XLA Ops:
  6.5 1.0 copy-start
  6.5 196.7 %all-reduce.6.cloned.1.call-start = ((), (), s32[]{:S(2)}) async-start(), calls=%async_computation | async-start | bytes 524288 | tf_op jit(solution)/shard_map/psum | solution.py:45
  8.8 454.2 %all-reduce.8.cloned.1.call-start = ((), (), s32[]{:S(2)}) async-start(), calls=%async_computation.1 | async-start | bytes 524288 | tf_op jit(solution)/shard_map/psum | solution.py:45
  203.3 2.6 copy-start.1
  269.9 8.0 collective-permute-start
  279.1 443.8 %all-reduce.10.cloned.1.call-start = ((), (), s32[]{:S(2)}) async-start(), calls=%async_computation.2 | async-start | bytes 524288 | tf_op jit(solution)/shard_map/psum | solution.py:45
  463.0 2.6 copy-start.2
  529.9 8.0 collective-permute-start.1
  539.0 444.0 %all-reduce.12.cloned.1.call-start = ((), (), s32[]{:S(2)}) async-start(), calls=%async_computation.3 | async-start | bytes 524288 | tf_op jit(solution)/shard_map/psum | solution.py:45
  722.8 2.6 copy-start.3
  790.0 8.0 collective-permute-start.2
  983.0 2.6 copy-start.4
  1049.9 14.8 %collective-permute-start.3 = (f32[256,128]{0,1:T(8,128)S(1)}, f32[256,128]{0,1:T(8,128)S(1)}, u32[]{:S(2)}, u32[]{:S(2)}) collective-permute-start(f32[256,128]{0,1:T(8,128)S(1)} %get-tuple-element.109), channel_id=1, source_target_pairs={{0,320},{64,384},{128,448},{192,0},{256,64},{320,128},{384,192},{4... | collective-permute-start | bytes 393224 | tf_op jit(solution)/shard_map/ppermute | solution.py:11
Sparse Core Ops, SparseCore 0:
  10.8 192.3 all-reduce.5
  279.2 183.7 all-reduce.7
  539.1 183.6 all-reduce.9
  799.2 183.7 all-reduce.11
where the time goes:
time: 1080 us; the launch traced here: 1070 us
  waiting for transfers between devices  769 us (71%)
  other arithmetic  218 us (20%)
  local copies, waits for them, and re-layouts  29.4 us (3%)
  matrix products  19.6 us (2%)
  between operations  19.4 us (2%)
  starting transfers between devices  15.7 us (1%)
    psum x4, waiting for transfers between devices, full_gram(): return lax.psum(inner_rows(paired, paired), 'row')  746 us
    another operation x27, other arithmetic, rotation(): lower_factor = jnp.linalg.cholesky(normal_matrix)  138 us
    another operation x9, other arithmetic, rotation(): lax.linalg.triangular_solve(lower_factor, partial_solve, left_side=True,...  78.8 us
    ppermute x4, waiting for transfers between devices, passed_along(): lax.ppermute(x, axis, [(i, (i + by) % length) for i in range(length)])  23.1 us
  transfers between devices with their start and end apart: 8, of which 8 were waited for; matrix products, arithmetic and copies ran while one was open for 0% of the time, Pallas kernels for 0%

commit v1 on v0

v1 whole, which is shorter than its diff:
```python
import functools

import jax
import jax.numpy as jnp
from jax import lax
from jax.experimental import pallas as pl
from jax.experimental.pallas import tpu as pltpu
from jax.sharding import PartitionSpec as P

ROUNDS = 4
BLOCK = 128
MESH = pl.DeviceIdType.MESH
F32 = jnp.float32
BF16 = jnp.bfloat16
SERIES_TOL = 1e-7
NEWTON_STEPS = 17


def dims(trans_a, trans_b):
    return (((0 if trans_a else 1,), (1 if trans_b else 0,)), ((), ()))


def dot1(a, b, trans_a=False):
    return lax.dot_general(a.astype(BF16), b.astype(BF16), dims(trans_a, False), preferred_element_type=F32)


def split(x):
    high = x.astype(BF16)
    return high, (x - high.astype(F32)).astype(BF16)


def dot3(a, b, trans_a=False):
    a_high, a_low = split(a)
    b_high, b_low = split(b)
    d = functools.partial(lax.dot_general, dimension_numbers=dims(trans_a, False), preferred_element_type=F32)
    return d(a_high, b_high) + (d(a_high, b_low) + d(a_low, b_high))


def dot6(a, b):
    return lax.dot_general(a, b, dims(False, False), precision=lax.Precision.HIGHEST, preferred_element_type=F32)


def iotas(shape):
    return lax.broadcasted_iota(jnp.int32, shape, 0), lax.broadcasted_iota(jnp.int32, shape, 1)


def half_generator(uu, ul, ll):
    rows, cols = iotas((BLOCK, BLOCK))
    eye = rows == cols
    half_sign = jnp.where(rows < cols, 0.5, jnp.where(rows > cols, -0.5, 0.0)).astype(F32)

    def norms(block):
        only = jnp.where(eye, block, 0.0)
        return jnp.sum(only, axis=1, keepdims=True), jnp.sum(only, axis=0, keepdims=True)

    u_col, u_row = norms(uu)
    l_col, l_row = norms(ll)
    a_uu = half_sign * uu / (u_col + u_row + 1e-06)
    a_ll = half_sign * ll / (l_col + l_row + 1e-06)
    a_ul = 0.5 * ul / (u_col + l_row + 1e-06)
    top = jnp.concatenate([a_uu, a_ul], axis=1)
    low = jnp.concatenate([-a_ul.T, a_ll], axis=1)
    return jnp.concatenate([top, low], axis=0)


def series_turn(a):
    a2 = dot3(a, a)
    both = dot1(jnp.concatenate([a, a2], axis=0), a2)
    width = a.shape[0]
    a3, a4 = both[:width], both[width:]
    first = a + a2 + a3
    turn = 2.0 * (first + (a4 + dot1(first, a4)))
    return turn, jnp.sum(a4 * a4, keepdims=True)


def newton_turn(a, scratch):
    width = a.shape[0]
    rows, cols = iotas((width, width))
    eye = (rows == cols).astype(F32)
    a2 = dot6(a, a)
    bound = jnp.max(jnp.sum(jnp.abs(a2), axis=1, keepdims=True), axis=0, keepdims=True)
    scratch[0] = eye - a
    scratch[1] = (eye + a) * (2.0 / (2.0 + bound))

    def step(_, carry):
        x = scratch[1]
        residual = (rows == cols).astype(F32) - dot6(scratch[0], x)
        scratch[1] = x + dot6(x, residual)
        return carry

    lax.fori_loop(0, NEWTON_STEPS, step, 0)
    return 2.0 * (scratch[1] - eye)


def kernel(n_wide, n_near, n_far, series, x_ref, out_ref, flag_ref,
           sent0, near0, far0, whole0, sent, near, far, whole,
           low_out, low_in, gram_out, gram_in, last_out, last_in, flag_out, flags, newton,
           send_sem, recv_sem, shift_send, shift_recv, last_send, last_recv, flag_send, flag_recv):
    wide, row = lax.axis_index("wide"), lax.axis_index("row")
    me_near, me_far = lax.rem(row, n_near), lax.div(row, n_near)

    def near_peer(k):
        other = lax.rem(me_near + k, n_near)
        return other, {"row": me_far * n_near + other}

    def far_peer(k):
        return {"row": lax.rem(me_far + k, n_far) * n_near + me_near}

    def wide_peer(k):
        return {"wide": lax.rem(wide + (k + n_wide), n_wide)}

    barrier = pltpu.get_barrier_semaphore()
    for k in range(1, n_near):
        pl.semaphore_signal(barrier, inc=1, device_id=near_peer(k)[1], device_id_type=MESH)
    for k in range(1, n_far):
        pl.semaphore_signal(barrier, inc=1, device_id=far_peer(k), device_id_type=MESH)
    for k in range(1, n_wide):
        pl.semaphore_signal(barrier, inc=1, device_id=wide_peer(k), device_id_type=MESH)

    sends = []

    def send(src, dst, ssem, rsem, peer):
        copy = pltpu.make_async_remote_copy(
            src_ref=src, dst_ref=dst, send_sem=ssem, recv_sem=rsem, device_id=peer, device_id_type=MESH
        )
        copy.start()
        sends.append(copy)
        return copy

    def reduce_rows(r, out, near_buf, far_buf, whole_buf):
        copies = []
        for k in range(1, n_near):
            other, peer = near_peer(k)
            copies.append(send(out.at[other], near_buf.at[me_near], send_sem.at[r, 0, k], recv_sem.at[r, 0, k], peer))
        near_buf[me_near] = out[me_near]
        for copy in copies:
            copy.wait_recv()
        total = near_buf[0]
        for i in range(1, n_near):
            total = total + near_buf[i]
        far_buf[me_far] = total
        copies = [
            send(far_buf.at[me_far], far_buf.at[me_far], send_sem.at[r, 1, k], recv_sem.at[r, 1, k], far_peer(k))
            for k in range(1, n_far)
        ]
        for copy in copies:
            copy.wait_recv()
        total = far_buf[0]
        for i in range(1, n_far):
            total = total + far_buf[i]
        whole_buf[me_near] = total
        copies = [
            send(whole_buf.at[me_near], whole_buf.at[me_near], send_sem.at[r, 2, k], recv_sem.at[r, 2, k],
                 near_peer(k)[1])
            for k in range(1, n_near)
        ]
        return copies

    upper, lower = x_ref[:, :BLOCK], x_ref[:, BLOCK:]
    local = dot3(jnp.concatenate([upper, lower], axis=1), jnp.concatenate([upper, lower], axis=1), True)
    payload = jnp.concatenate([local[:BLOCK, BLOCK:], local[:BLOCK, :BLOCK], local[BLOCK:, BLOCK:]], axis=0)
    sent0[...] = payload.reshape(sent0.shape)
    pl.semaphore_wait(barrier, (n_near - 1) + (n_far - 1) + (n_wide - 1))

    worst = jnp.zeros((1, 1), F32)
    for r in range(ROUNDS):
        if r == 0:
            copies = reduce_rows(0, sent0, near0, far0, whole0)
            for copy in copies:
                copy.wait_recv()
            gram = whole0[...].reshape(3 * BLOCK, BLOCK)
            ul, uu, ll = gram[:BLOCK], gram[BLOCK:2 * BLOCK], gram[2 * BLOCK:]
        else:
            copies = reduce_rows(r, sent.at[r - 1], near.at[r - 1], far.at[r - 1], whole.at[r - 1])
            for copy in copies:
                copy.wait_recv()
            gram_copy.wait_recv()
            ul = whole[r - 1].reshape(BLOCK, BLOCK)
            uu, ll = kept_uu, gram_in[r - 1]
        a = half_generator(uu, ul, ll)
        if series:
            turn, rest = series_turn(a)
            worst = jnp.maximum(worst, rest)
        else:
            turn = newton_turn(a, newton)
        pair = jnp.concatenate([upper, lower], axis=1)
        turned = pair + dot3(pair, turn)
        upper = turned[:, :BLOCK]
        if r == ROUNDS - 1:
            last_out[...] = turned[:, BLOCK:]
            last = send(last_out, last_in, last_send, last_recv, wide_peer(-(ROUNDS - 1)))
            out_ref[:, :BLOCK] = upper
            break
        low_out[r] = turned[:, BLOCK:]
        low_copy = send(low_out.at[r], low_in.at[r], shift_send.at[r, 0], shift_recv.at[r, 0], wide_peer(1))
        full = jnp.concatenate(
            [jnp.concatenate([uu, ul], axis=1), jnp.concatenate([ul.T, ll], axis=1)], axis=0
        )
        half = full + dot3(full, turn)
        left, right = half[:, :BLOCK], half[:, BLOCK:]
        kept_uu = left[:BLOCK] + dot3(turn[:, :BLOCK], left, True)
        gram_out[r] = right[BLOCK:] + dot3(turn[:, BLOCK:], right, True)
        gram_copy = send(gram_out.at[r], gram_in.at[r], shift_send.at[r, 1], shift_recv.at[r, 1], wide_peer(1))
        low_copy.wait_recv()
        lower = low_in[r]
        sent[r] = dot3(upper, lower, True).reshape(sent.shape[1:])

    if series:
        flag_out[...] = jnp.broadcast_to(worst, flag_out.shape)
        flags[wide] = flag_out[...]
        copies = [
            send(flag_out, flags.at[wide], flag_send.at[k], flag_recv.at[k], wide_peer(k)) for k in range(1, n_wide)
        ]
        for copy in copies:
            copy.wait_recv()
        flag_ref[...] = jnp.max(flags[...], axis=0)
    else:
        flag_ref[...] = jnp.zeros_like(flag_ref)
    last.wait_recv()
    out_ref[:, BLOCK:] = last_in[...]
    for copy in sends:
        copy.wait_send()


def run(columns, sizes, series, collective_id):
    n_wide, n_near, n_far = sizes
    rows = columns.shape[0]
    first, later = 3 * BLOCK // n_near, BLOCK // n_near
    count = ROUNDS - 1
    vmem = lambda *shape: pltpu.VMEM(shape, F32)
    sems = pltpu.SemaphoreType.DMA
    peers = max(n_near, n_far)
    return pl.pallas_call(
        functools.partial(kernel, n_wide, n_near, n_far, series),
        out_shape=(
            jax.ShapeDtypeStruct(columns.shape, F32),
            jax.ShapeDtypeStruct((8, BLOCK), F32),
        ),
        in_specs=[pl.BlockSpec(memory_space=pltpu.VMEM)],
        out_specs=(pl.BlockSpec(memory_space=pltpu.VMEM), pl.BlockSpec(memory_space=pltpu.VMEM)),
        scratch_shapes=[
            vmem(n_near, first, BLOCK), vmem(n_near, first, BLOCK), vmem(n_far, first, BLOCK),
            vmem(n_near, first, BLOCK),
            vmem(count, n_near, later, BLOCK), vmem(count, n_near, later, BLOCK), vmem(count, n_far, later, BLOCK),
            vmem(count, n_near, later, BLOCK),
            vmem(count, rows, BLOCK), vmem(count, rows, BLOCK),
            vmem(count, BLOCK, BLOCK), vmem(count, BLOCK, BLOCK),
            vmem(rows, BLOCK), vmem(rows, BLOCK),
            vmem(8, BLOCK), vmem(n_wide, 8, BLOCK), vmem(2, 2 * BLOCK, 2 * BLOCK),
            sems((ROUNDS, 3, peers)), sems((ROUNDS, 3, peers)),
            sems((count, 2)), sems((count, 2)), sems, sems, sems((n_wide,)), sems((n_wide,)),
        ],
        compiler_params=pltpu.CompilerParams(collective_id=collective_id, has_side_effects=True),
        name="jacobi_series" if series else "jacobi_newton",
    )(columns)


def per_device(sizes, columns):
    fast, rest = run(columns, sizes, True, 0)
    return lax.cond(
        jnp.logical_not(rest[0, 0] <= SERIES_TOL),
        lambda x, y: run(x, sizes, False, 1)[0],
        lambda x, y: y,
        columns, fast,
    )


def solution(mesh, n_near=8):
    sizes = (mesh.shape["wide"], n_near, mesh.shape["row"] // n_near)
    return jax.shard_map(
        functools.partial(per_device, sizes),
        mesh=mesh,
        in_specs=(P("row", "wide"),),
        out_specs=P("row", "wide"),
        check_vma=False,
    )
```

time: 1080 us -> 277 us (0.26)
  waiting for transfers between devices: 769 us -> 0 us
  Pallas kernels: 0 us -> 270 us
  other arithmetic: 218 us -> 0 us
  local copies, waits for them, and re-layouts: 29.4 us -> 1.89 us
  matrix products: 19.6 us -> 0 us
  between operations: 19.4 us -> 0.68 us
  starting transfers between devices: 15.7 us -> 0 us
    psum x4 -> x0, waiting for transfers between devices: 746 us -> none  [full_gram(): return lax.psum(inner_rows(paired, paired), 'row')]
    pallas_call x0 -> x2, Pallas kernels: none -> 270 us  [run(): pl.pallas_call(functools.partial(kernel, n_wide, n_near, n_far, series),...]
    another operation x36 -> x0, other arithmetic: 217 us -> none  [the longest x27 138 us: rotation(): lower_factor = jnp.linalg.cholesky(normal_matrix)]
    ppermute x4 -> x0, waiting for transfers between devices: 23.1 us -> none  [passed_along(): lax.ppermute(x, axis, [(i, (i + by) % length) for i in range(length)])]
    another operation x37 -> x0, local copies, waits for them, and re-layouts: 16.4 us -> none  [the longest x29 16.3 us: rotation(): lax.linalg.triangular_solve(lower_factor, partial_solve, left_side=True,...]
    ppermute x4 -> x0, starting transfers between devices: 15.6 us -> none  [passed_along(): lax.ppermute(x, axis, [(i, (i + by) % length) for i in range(length)])]
    dot_general x16 -> x0, matrix products: 10.9 us -> none  [the longest x4 4.63 us: inner_rows(): lax.dot_general(left, right, (((0,), (0,)), ((), ())), precision=lax.Prec...]
  transfers between devices with their start and end apart: 8 -> 0, of which waited for: 8 -> 0; matrix products, arithmetic and copies ran while one was open for 0% -> 0% of each run, Pallas kernels for 0% -> 0%
where the time goes in v1:
time: 277 us; the launch traced here: 273 us
  Pallas kernels  270 us (97%)
    pallas_call x2, Pallas kernels, run(): pl.pallas_call(functools.partial(kernel, n_wide, n_near, n_far, series),...  270 us

profile of v1, /device:TPU:1, one launch (start us, length us, event | category | flops | bytes accessed | tf_op | source)
XLA Modules:
  0.0 273.0 jit_solution(11013323292286484700)
XLA Ops:
  0.0 0.0 copy-start
  0.0 104.3 %jacobi_series.1 = (f32[256,256]{1,0:T(8,128)S(1)}, f32[8,128]{1,0:T(8,128)}) custom-call(f32[256,256]{1,0:T(8,128)} %x_ref.2), custom_call_target="tpu_custom_call" | custom-call | tf_op jit(solution)/shard_map/jacobi_series/pallas_call | solution.py:233
  104.3 1.2 slice.3
  106.1 0.0 copy-done
  106.1 166.1 %conditional.1 = (f32[256,256]{1,0:T(8,128)S(1)}) conditional(s32[]{:T(128)} %bitcast, f32[256,256]{1,0:T(8,128)S(1)} %get-tuple-element.14, f32[256,256]{1,0:T(8,128)S(1)} %copy-done), branch_computations={%region_0.0_spmd, %region_1.0_spmd} | conditional | bytes 8 | solution.py:260
  106.3 165.9 %jacobi_newton.1 = (f32[256,256]{1,0:T(8,128)S(1)}, f32[8,128]{1,0:T(8,128)}) custom-call(f32[256,256]{1,0:T(8,128)S(1)} %x_ref.1), custom_call_target="tpu_custom_call" | custom-call | tf_op jit(solution)/shard_map/cond/branch_1_fun/jacobi_newton/pallas_call | solution.py:233
  272.3 0.7 copy.7
Async XLA Ops:
  0.0 106.1 %copy-start = (f32[256,256]{1,0:T(8,128)S(1)}, f32[256,256]{1,0:T(8,128)}, u32[]{:S(2)}) copy-start(f32[256,256]{1,0:T(8,128)} %x_ref.2) | copy-start | bytes 786436

commit v2 on v1

--- a/solution.py
+++ b/solution.py
@@ -12,7 +12,7 @@
 MESH = pl.DeviceIdType.MESH
 F32 = jnp.float32
 BF16 = jnp.bfloat16
-SERIES_TOL = 1e-7
+SERIES_TOL = 1e-12
 NEWTON_STEPS = 17
 
 
@@ -69,8 +69,10 @@
     width = a.shape[0]
     a3, a4 = both[:width], both[width:]
     first = a + a2 + a3
-    turn = 2.0 * (first + (a4 + dot1(first, a4)))
-    return turn, jnp.sum(a4 * a4, keepdims=True)
+    both = dot1(jnp.concatenate([first, a4], axis=0), a4)
+    rest, a8 = both[:width], both[width:]
+    turn = 2.0 * (first + (a4 + (rest + a8)))
+    return turn, jnp.sum(a8 * a8, keepdims=True) * jnp.sum(a * a, keepdims=True)
 
 
 def newton_turn(a, scratch):
@@ -213,9 +215,9 @@
         ]
         for copy in copies:
             copy.wait_recv()
-        flag_ref[...] = jnp.max(flags[...], axis=0)
+        flag_ref[0, 0] = jnp.max(jnp.where(flags[...] <= SERIES_TOL, 0, 1))
     else:
-        flag_ref[...] = jnp.zeros_like(flag_ref)
+        flag_ref[0, 0] = 0
     last.wait_recv()
     out_ref[:, BLOCK:] = last_in[...]
     for copy in sends:
@@ -234,10 +236,10 @@
         functools.partial(kernel, n_wide, n_near, n_far, series),
         out_shape=(
             jax.ShapeDtypeStruct(columns.shape, F32),
-            jax.ShapeDtypeStruct((8, BLOCK), F32),
+            jax.ShapeDtypeStruct((1, 1), jnp.int32),
         ),
         in_specs=[pl.BlockSpec(memory_space=pltpu.VMEM)],
-        out_specs=(pl.BlockSpec(memory_space=pltpu.VMEM), pl.BlockSpec(memory_space=pltpu.VMEM)),
+        out_specs=(pl.BlockSpec(memory_space=pltpu.VMEM), pl.BlockSpec(memory_space=pltpu.SMEM)),
         scratch_shapes=[
             vmem(n_near, first, BLOCK), vmem(n_near, first, BLOCK), vmem(n_far, first, BLOCK),
             vmem(n_near, first, BLOCK),
@@ -256,11 +258,10 @@
 
 
 def per_device(sizes, columns):
-    fast, rest = run(columns, sizes, True, 0)
-    return lax.cond(
-        jnp.logical_not(rest[0, 0] <= SERIES_TOL),
-        lambda x, y: run(x, sizes, False, 1)[0],
-        lambda x, y: y,
+    fast, short = run(columns, sizes, True, 0)
+    return lax.switch(
+        short[0, 0],
+        [lambda x, y: y, lambda x, y: run(x, sizes, False, 1)[0]],
         columns, fast,
     )
 

time: 277 us -> 276 us (level)
  no operation moved by 1% of the time
where the time goes in v2:
time: 276 us; the launch traced here: 272 us
  Pallas kernels  271 us (98%)
    pallas_call x2, Pallas kernels, run(): pl.pallas_call(functools.partial(kernel, n_wide, n_near, n_far, series),...  271 us

profile of v2, /device:TPU:1, one launch (start us, length us, event | category | flops | bytes accessed | tf_op | source)
XLA Modules:
  0.0 272.1 jit_solution(11146081181613463573)
XLA Ops:
  0.0 0.0 copy-start
  0.0 104.8 %jacobi_series.1 = (f32[256,256]{1,0:T(8,128)S(1)}, s32[1,1]{1,0:T(1,128)}) custom-call(f32[256,256]{1,0:T(8,128)} %x_ref.2), custom_call_target="tpu_custom_call" | custom-call | tf_op jit(solution)/shard_map/jacobi_series/pallas_call | solution.py:235
  105.4 0.0 copy-done
  105.4 166.0 %conditional.1 = (f32[256,256]{1,0:T(8,128)S(1)}) conditional(s32[]{:T(128)} %bitcast, f32[256,256]{1,0:T(8,128)S(1)} %get-tuple-element.14, f32[256,256]{1,0:T(8,128)S(1)} %copy-done), branch_computations={%region_0.0_spmd, %region_1.0_spmd} | conditional | bytes 8 | solution.py:262
  105.6 165.8 %jacobi_newton.1 = (f32[256,256]{1,0:T(8,128)S(1)}, s32[1,1]{1,0:T(1,128)}) custom-call(f32[256,256]{1,0:T(8,128)S(1)} %x_ref.1), custom_call_target="tpu_custom_call" | custom-call | tf_op jit(solution)/shard_map/cond/branch_1_fun/jacobi_newton/pallas_call | solution.py:235
  271.4 0.7 copy.7
Async XLA Ops:
  0.0 105.4 %copy-start = (f32[256,256]{1,0:T(8,128)S(1)}, f32[256,256]{1,0:T(8,128)}, u32[]{:S(2)}) copy-start(f32[256,256]{1,0:T(8,128)} %x_ref.2) | copy-start | bytes 786436

commit v3 on v2

v3 whole, which is shorter than its diff:
```python
import functools

import jax
import jax.numpy as jnp
from jax import lax
from jax.experimental import pallas as pl
from jax.experimental.pallas import tpu as pltpu
from jax.sharding import PartitionSpec as P

BLOCK = 128
MESH = pl.DeviceIdType.MESH
F32 = jnp.float32
BF16 = jnp.bfloat16
SERIES_TOL = 1e-12
NEWTON_STEPS = 17


def dims(trans_a, trans_b):
    return (((0 if trans_a else 1,), (1 if trans_b else 0,)), ((), ()))


def dot1(a, b, trans_a=False):
    return lax.dot_general(a.astype(BF16), b.astype(BF16), dims(trans_a, False), preferred_element_type=F32)


def split(x):
    high = x.astype(BF16)
    return high, (x - high.astype(F32)).astype(BF16)


def dot3(a, b, trans_a=False):
    a_high, a_low = split(a)
    b_high, b_low = split(b)
    d = functools.partial(lax.dot_general, dimension_numbers=dims(trans_a, False), preferred_element_type=F32)
    return d(a_high, b_high) + (d(a_high, b_low) + d(a_low, b_high))


def dot6(a, b):
    return lax.dot_general(a, b, dims(False, False), precision=lax.Precision.HIGHEST, preferred_element_type=F32)


def iotas(shape):
    return lax.broadcasted_iota(jnp.int32, shape, 0), lax.broadcasted_iota(jnp.int32, shape, 1)


def half_generator(uu, ul, ll):
    rows, cols = iotas((BLOCK, BLOCK))
    eye = rows == cols
    half_sign = jnp.where(rows < cols, 0.5, jnp.where(rows > cols, -0.5, 0.0)).astype(F32)

    def norms(block):
        only = jnp.where(eye, block, 0.0)
        return jnp.sum(only, axis=1, keepdims=True), jnp.sum(only, axis=0, keepdims=True)

    u_col, u_row = norms(uu)
    l_col, l_row = norms(ll)
    a_uu = half_sign * uu / (u_col + u_row + 1e-06)
    a_ll = half_sign * ll / (l_col + l_row + 1e-06)
    a_ul = 0.5 * ul / (u_col + l_row + 1e-06)
    top = jnp.concatenate([a_uu, a_ul], axis=1)
    low = jnp.concatenate([-a_ul.T, a_ll], axis=1)
    return jnp.concatenate([top, low], axis=0)


def series_turn(a):
    a2 = dot3(a, a)
    both = dot1(jnp.concatenate([a, a2], axis=0), a2)
    width = a.shape[0]
    a3, a4 = both[:width], both[width:]
    first = a + a2 + a3
    both = dot1(jnp.concatenate([first, a4], axis=0), a4)
    rest, a8 = both[:width], both[width:]
    turn = 2.0 * (first + (a4 + (rest + a8)))
    return turn, jnp.sum(a8 * a8, keepdims=True) * jnp.sum(a * a, keepdims=True)


def newton_turn(a, scratch):
    width = a.shape[0]
    rows, cols = iotas((width, width))
    eye = (rows == cols).astype(F32)
    a2 = dot6(a, a)
    bound = jnp.max(jnp.sum(jnp.abs(a2), axis=1, keepdims=True), axis=0, keepdims=True)
    scratch[0] = eye - a
    scratch[1] = (eye + a) * (2.0 / (2.0 + bound))

    def step(_, carry):
        x = scratch[1]
        residual = (rows == cols).astype(F32) - dot6(scratch[0], x)
        scratch[1] = x + dot6(x, residual)
        return carry

    lax.fori_loop(0, NEWTON_STEPS, step, 0)
    return 2.0 * (scratch[1] - eye)


def kernel(n_wide, n_near, n_far, series, x_hbm, out_ref, flag_ref, x_ref, *refs):
    (reduces, (next_x, turn_out, turn_in, gram_out, gram_in, up_out, up_in, upgram_out, upgram_in, low_out, low_in,
               last_low_out, last_low_in, last_up_out, last_up_in, flag_out, flags, newton),
     (reduce_send, reduce_recv, move_send, move_recv, flag_send, flag_recv, load_sem)) = (
        [refs[4 * i:4 * i + 4] for i in range(4)], refs[16:34], refs[34:])
    wide, row = lax.axis_index("wide"), lax.axis_index("row")
    me_near, me_far = lax.rem(row, n_near), lax.div(row, n_near)

    def near_peer(k):
        other = lax.rem(me_near + k, n_near)
        return other, {"row": me_far * n_near + other}

    def far_peer(k):
        return {"row": lax.rem(me_far + k, n_far) * n_near + me_near}

    def wide_peer(k):
        return {"wide": lax.rem(wide + (k + n_wide), n_wide)}

    load = pltpu.make_async_copy(x_hbm, x_ref, load_sem)
    load.start()
    barrier = pltpu.get_barrier_semaphore()
    for k in range(1, n_near):
        pl.semaphore_signal(barrier, inc=1, device_id=near_peer(k)[1], device_id_type=MESH)
    for k in range(1, n_wide):
        pl.semaphore_signal(barrier, inc=1, device_id=wide_peer(k), device_id_type=MESH)
    for k in range(1, n_far):
        pl.semaphore_signal(barrier, inc=1, device_id=far_peer(k), device_id_type=MESH)

    sends = []

    def send(src, dst, ssem, rsem, peer):
        copy = pltpu.make_async_remote_copy(
            src_ref=src, dst_ref=dst, send_sem=ssem, recv_sem=rsem, device_id=peer, device_id_type=MESH
        )
        copy.start()
        sends.append(copy)
        return copy

    def move(i, src, dst, by):
        return send(src, dst, move_send.at[i], move_recv.at[i], wide_peer(by))

    def arrived(copies):
        for copy in copies:
            copy.wait_recv()

    def total(buf, count):
        value = buf[0]
        for i in range(1, count):
            value = value + buf[i]
        return value

    def scatter(i, payload):
        out, near, far, whole = reduces[i]
        out[...] = payload.reshape(out.shape)
        copies = []
        for k in range(1, n_near):
            other, peer = near_peer(k)
            copies.append(
                send(out.at[other], near.at[me_near], reduce_send.at[i, 0, k], reduce_recv.at[i, 0, k], peer))
        near[me_near] = out[me_near]
        return copies

    def across(i, copies):
        out, near, far, whole = reduces[i]
        arrived(copies)
        far[me_far] = total(near, n_near)
        return [
            send(far.at[me_far], far.at[me_far], reduce_send.at[i, 1, k], reduce_recv.at[i, 1, k], far_peer(k))
            for k in range(1, n_far)
        ]

    def gather(i, copies):
        out, near, far, whole = reduces[i]
        arrived(copies)
        whole[me_near] = total(far, n_far)
        return [
            send(whole.at[me_near], whole.at[me_near], reduce_send.at[i, 2, k], reduce_recv.at[i, 2, k],
                 near_peer(k)[1])
            for k in range(1, n_near)
        ]

    def reduced(i, copies):
        arrived(copies)
        whole = reduces[i][3]
        return whole[...].reshape(-1, BLOCK)

    def blocks(m):
        return jnp.concatenate([m[:BLOCK, :BLOCK], m[:BLOCK, BLOCK:], m[BLOCK:, :BLOCK], m[BLOCK:, BLOCK:]], axis=0)

    def joined(uu, ul, lu, ll):
        return jnp.concatenate(
            [jnp.concatenate([uu, ul], axis=1), jnp.concatenate([lu, ll], axis=1)], axis=0)

    worst = jnp.zeros((1, 1), F32)

    def turn_of(uu, ul, ll):
        nonlocal worst
        a = half_generator(uu, ul, ll)
        if series:
            turn, rest = series_turn(a)
            worst = jnp.maximum(worst, rest)
        else:
            turn = newton_turn(a, newton)
        return turn

    def first_round(s, pair, uu, ul, ll):
        turn = turn_of(uu, ul, ll)
        turn_out[s] = turn[:, BLOCK:]
        turn_copy = move(2 * s, turn_out.at[s], turn_in.at[s], 1)
        full = joined(uu, ul, ul.T, ll)
        half = full + dot3(full, turn)
        gram_out[s] = half[BLOCK:, BLOCK:] + dot3(turn[:, BLOCK:], half[:, BLOCK:], True)
        gram_copy = move(2 * s + 1, gram_out.at[s], gram_in.at[s], 1)
        next_uu = half[:BLOCK, :BLOCK] + dot3(turn[:, :BLOCK], half[:, :BLOCK], True)
        upper = pair[:, :BLOCK] + dot3(pair, turn[:, :BLOCK])
        return turn[:, :BLOCK], upper, next_uu, turn_copy, gram_copy

    def cross_gram(s, left_turn, cross):
        right_turn = turn_in[s]
        half = cross[:, BLOCK:] + dot3(cross, right_turn)
        return half[:BLOCK] + dot3(left_turn, half, True)

    load.wait()
    pair = x_ref[...]
    local = dot3(pair, pair, True)
    payload = jnp.concatenate([local[:BLOCK, BLOCK:], local[:BLOCK, :BLOCK], local[BLOCK:, BLOCK:]], axis=0)
    pl.semaphore_wait(barrier, (n_near - 1) + (n_far - 1) + (n_wide - 1))
    grams = scatter(0, payload)
    next_copy = move(4, x_ref, next_x, 1)
    grams = across(0, grams)
    next_copy.wait_recv()
    next_pair = next_x[...]
    crosses = scatter(1, blocks(dot3(pair, next_pair, True)))
    grams = gather(0, grams)
    crosses = across(1, crosses)
    gram = reduced(0, grams)
    left_turn, upper, uu, turn_copy, gram_copy = first_round(
        0, pair, gram[BLOCK:2 * BLOCK], gram[:BLOCK], gram[2 * BLOCK:])
    crosses = gather(1, crosses)
    turn_copy.wait_recv()
    right_turn = turn_in[0]
    lower = next_pair[:, BLOCK:] + dot3(next_pair, right_turn)
    pair = jnp.concatenate([upper, lower], axis=1)
    gram_copy.wait_recv()
    cross = reduced(1, crosses)
    cross = joined(cross[:BLOCK], cross[BLOCK:2 * BLOCK], cross[2 * BLOCK:3 * BLOCK], cross[3 * BLOCK:])
    ul, ll = cross_gram(0, left_turn, cross), gram_in[0]
    turn = turn_of(uu, ul, ll)
    up_out[...] = pair[:, :BLOCK] + dot3(pair, turn[:, :BLOCK])
    up_copy = move(5, up_out, up_in, -1)
    low_out[...] = pair[:, BLOCK:] + dot3(pair, turn[:, BLOCK:])
    low_copy = move(6, low_out, low_in, 1)
    full = joined(uu, ul, ul.T, ll)
    half = full + dot3(full, turn)
    upgram_out[...] = half[:BLOCK, :BLOCK] + dot3(turn[:, :BLOCK], half[:, :BLOCK], True)
    upgram_copy = move(7, upgram_out, upgram_in, -1)
    ll = half[BLOCK:, BLOCK:] + dot3(turn[:, BLOCK:], half[:, BLOCK:], True)

    kept_up, kept_low = up_out[...], low_out[...]
    low_up = dot3(kept_low, kept_up, True)
    up_copy.wait_recv()
    upper = up_in[...]
    grams = scatter(2, dot3(kept_low, upper, True))
    up_up = dot3(upper, kept_up, True)
    low_copy.wait_recv()
    next_low = low_in[...]
    next_pair = jnp.concatenate([kept_up, next_low], axis=1)
    pair = jnp.concatenate([upper, kept_low], axis=1)
    right = dot3(pair, next_low, True)
    crosses = scatter(3, jnp.concatenate([up_up, right[:BLOCK], low_up, right[BLOCK:]], axis=0))
    grams = across(2, grams)
    crosses = across(3, crosses)
    grams = gather(2, grams)
    upgram_copy.wait_recv()
    ul = reduced(2, grams).T
    left_turn, upper, uu, turn_copy, gram_copy = first_round(1, pair, upgram_in[...], ul, ll)
    crosses = gather(3, crosses)
    turn_copy.wait_recv()
    right_turn = turn_in[1]
    lower = next_pair[:, BLOCK:] + dot3(next_pair, right_turn)
    pair = jnp.concatenate([upper, lower], axis=1)
    gram_copy.wait_recv()
    cross = reduced(3, crosses)
    cross = joined(cross[:BLOCK], cross[BLOCK:2 * BLOCK], cross[2 * BLOCK:3 * BLOCK], cross[3 * BLOCK:])
    turn = turn_of(uu, cross_gram(1, left_turn, cross), gram_in[1])
    last_low_out[...] = pair[:, BLOCK:] + dot3(pair, turn[:, BLOCK:])
    last_low = move(8, last_low_out, last_low_in, -2)
    last_up_out[...] = pair[:, :BLOCK] + dot3(pair, turn[:, :BLOCK])
    last_up = move(9, last_up_out, last_up_in, 1)

    if series:
        flag_out[...] = jnp.broadcast_to(worst, flag_out.shape)
        flags[wide] = flag_out[...]
        arrived([
            send(flag_out, flags.at[wide], flag_send.at[k], flag_recv.at[k], wide_peer(k)) for k in range(1, n_wide)
        ])
        flag_ref[0, 0] = jnp.max(jnp.where(flags[...] <= SERIES_TOL, 0, 1))
    else:
        flag_ref[0, 0] = 0
    last_up.wait_recv()
    out_ref[:, :BLOCK] = last_up_in[...]
    last_low.wait_recv()
    out_ref[:, BLOCK:] = last_low_in[...]
    for copy in sends:
        copy.wait_send()


def run(columns, sizes, series, collective_id):
    n_wide, n_near, n_far = sizes
    rows, width = columns.shape
    vmem = lambda *shape: pltpu.VMEM(shape, F32)
    sems = pltpu.SemaphoreType.DMA
    peers = max(n_near, n_far)
    scratch = [vmem(rows, width)]
    for count in (3, 4, 1, 4):
        piece = count * BLOCK // n_near
        scratch += [vmem(n, piece, BLOCK) for n in (n_near, n_near, n_far, n_near)]
    scratch += [
        vmem(rows, width),
        vmem(2, width, BLOCK), vmem(2, width, BLOCK), vmem(2, BLOCK, BLOCK), vmem(2, BLOCK, BLOCK),
        vmem(rows, BLOCK), vmem(rows, BLOCK), vmem(BLOCK, BLOCK), vmem(BLOCK, BLOCK),
        vmem(rows, BLOCK), vmem(rows, BLOCK),
        vmem(rows, BLOCK), vmem(rows, BLOCK), vmem(rows, BLOCK), vmem(rows, BLOCK),
        vmem(8, BLOCK), vmem(n_wide, 8, BLOCK), vmem(2, width, width),
        sems((4, 3, peers)), sems((4, 3, peers)), sems((10,)), sems((10,)), sems((n_wide,)), sems((n_wide,)), sems,
    ]
    return pl.pallas_call(
        functools.partial(kernel, n_wide, n_near, n_far, series),
        out_shape=(
            jax.ShapeDtypeStruct(columns.shape, F32),
            jax.ShapeDtypeStruct((1, 1), jnp.int32),
        ),
        in_specs=[pl.BlockSpec(memory_space=pl.ANY)],
        out_specs=(pl.BlockSpec(memory_space=pltpu.VMEM), pl.BlockSpec(memory_space=pltpu.SMEM)),
        scratch_shapes=scratch,
        compiler_params=pltpu.CompilerParams(collective_id=collective_id, has_side_effects=True),
        name="jacobi_series" if series else "jacobi_newton",
    )(columns)


def per_device(sizes, columns):
    fast, short = run(columns, sizes, True, 0)
    return lax.switch(
        short[0, 0],
        [lambda x, y: y, lambda x, y: run(x, sizes, False, 1)[0]],
        columns, fast,
    )


def solution(mesh, n_near=8):
    sizes = (mesh.shape["wide"], n_near, mesh.shape["row"] // n_near)
    return jax.shard_map(
        functools.partial(per_device, sizes),
        mesh=mesh,
        in_specs=(P("row", "wide"),),
        out_specs=P("row", "wide"),
        check_vma=False,
    )
```

time: 276 us -> 227 us (0.82); the launches traced: 272 us -> 227 us
  Pallas kernels: 271 us -> 225 us
    pallas_call x2, Pallas kernels: 271 us -> 225 us  [run(): pl.pallas_call(functools.partial(kernel, n_wide, n_near, n_far, series),...]
where the time goes in v3:
time: 227 us
  Pallas kernels  225 us (99%)
    pallas_call x2, Pallas kernels, run(): pl.pallas_call(functools.partial(kernel, n_wide, n_near, n_far, series),...  225 us

profile of v3, /device:TPU:1, one launch (start us, length us, event | category | flops | bytes accessed | tf_op | source)
XLA Modules:
  0.0 227.0 jit_solution(2758576448008281801)
XLA Ops:
  0.0 0.0 copy-start
  0.0 83.2 %jacobi_series.1 = (f32[256,256]{1,0:T(8,128)S(1)}, s32[1,1]{1,0:T(1,128)}) custom-call(f32[256,256]{1,0:T(8,128)} %x_hbm.2), custom_call_target="tpu_custom_call" | custom-call | tf_op jit(solution)/shard_map/jacobi_series/pallas_call | solution.py:322
  83.9 0.0 copy-done
  83.9 142.4 %conditional.1 = (f32[256,256]{1,0:T(8,128)S(1)}) conditional(s32[]{:T(128)} %bitcast, f32[256,256]{1,0:T(8,128)S(1)} %get-tuple-element.14, f32[256,256]{1,0:T(8,128)S(1)} %copy-done), branch_computations={%region_0.0_spmd, %region_1.0_spmd} | conditional | bytes 8 | solution.py:338
  84.1 142.2 %jacobi_newton.1 = (f32[256,256]{1,0:T(8,128)S(1)}, s32[1,1]{1,0:T(1,128)}) custom-call(f32[256,256]{1,0:T(8,128)S(1)} %x_hbm.1), custom_call_target="tpu_custom_call" | custom-call | tf_op jit(solution)/shard_map/cond/branch_1_fun/jacobi_newton/pallas_call | solution.py:322
  226.3 0.7 copy.7
Async XLA Ops:
  0.0 83.9 %copy-start = (f32[256,256]{1,0:T(8,128)S(1)}, f32[256,256]{1,0:T(8,128)}, u32[]{:S(2)}) copy-start(f32[256,256]{1,0:T(8,128)} %x_hbm.2) | copy-start | bytes 786436

commit v4 on v3

--- a/solution.py
+++ b/solution.py
@@ -94,10 +94,10 @@
 
 
 def kernel(n_wide, n_near, n_far, series, x_hbm, out_ref, flag_ref, x_ref, *refs):
-    (reduces, (next_x, turn_out, turn_in, gram_out, gram_in, up_out, up_in, upgram_out, upgram_in, low_out, low_in,
+    (reduces, (next_x, turn_out, turn_in, gram_out, gram_in, lowgram_out, lowgram_in, next_whole, up_out, up_in, upgram_out, upgram_in, low_out, low_in,
                last_low_out, last_low_in, last_up_out, last_up_in, flag_out, flags, newton),
-     (reduce_send, reduce_recv, move_send, move_recv, flag_send, flag_recv, load_sem)) = (
-        [refs[4 * i:4 * i + 4] for i in range(4)], refs[16:34], refs[34:])
+     (reduce_send, reduce_recv, move_send, move_recv, flag_send, flag_recv, next_send, next_recv, load_sem)) = (
+        [refs[4 * i:4 * i + 4] for i in range(6)], refs[24:45], refs[45:])
     wide, row = lax.axis_index("wide"), lax.axis_index("row")
     me_near, me_far = lax.rem(row, n_near), lax.div(row, n_near)
 
@@ -111,15 +111,21 @@
     def wide_peer(k):
         return {"wide": lax.rem(wide + (k + n_wide), n_wide)}
 
+    def next_near(k, by):
+        return near_peer(k)[1] | wide_peer(by)
+
     load = pltpu.make_async_copy(x_hbm, x_ref, load_sem)
     load.start()
     barrier = pltpu.get_barrier_semaphore()
+    for k in sorted(range(1, n_far), key=lambda k: abs(2 * k - n_far)):
+        pl.semaphore_signal(barrier, inc=1, device_id=far_peer(k), device_id_type=MESH)
+    for k in sorted(range(1, n_wide), key=lambda k: abs(2 * k - n_wide)):
+        pl.semaphore_signal(barrier, inc=1, device_id=wide_peer(k), device_id_type=MESH)
+    for k in range(1, n_near):
+        pl.semaphore_signal(barrier, inc=1, device_id=next_near(k, 1), device_id_type=MESH)
+        pl.semaphore_signal(barrier, inc=1, device_id=next_near(k, -1), device_id_type=MESH)
     for k in range(1, n_near):
         pl.semaphore_signal(barrier, inc=1, device_id=near_peer(k)[1], device_id_type=MESH)
-    for k in range(1, n_wide):
-        pl.semaphore_signal(barrier, inc=1, device_id=wide_peer(k), device_id_type=MESH)
-    for k in range(1, n_far):
-        pl.semaphore_signal(barrier, inc=1, device_id=far_peer(k), device_id_type=MESH)
 
     sends = []
 
@@ -179,9 +185,6 @@
         whole = reduces[i][3]
         return whole[...].reshape(-1, BLOCK)
 
-    def blocks(m):
-        return jnp.concatenate([m[:BLOCK, :BLOCK], m[:BLOCK, BLOCK:], m[BLOCK:, :BLOCK], m[BLOCK:, BLOCK:]], axis=0)
-
     def joined(uu, ul, lu, ll):
         return jnp.concatenate(
             [jnp.concatenate([uu, ul], axis=1), jnp.concatenate([lu, ll], axis=1)], axis=0)
@@ -198,97 +201,110 @@
             turn = newton_turn(a, newton)
         return turn
 
-    def first_round(s, pair, uu, ul, ll):
-        turn = turn_of(uu, ul, ll)
-        turn_out[s] = turn[:, BLOCK:]
-        turn_copy = move(2 * s, turn_out.at[s], turn_in.at[s], 1)
+    def turned(turn, uu, ul, ll):
         full = joined(uu, ul, ul.T, ll)
         half = full + dot3(full, turn)
-        gram_out[s] = half[BLOCK:, BLOCK:] + dot3(turn[:, BLOCK:], half[:, BLOCK:], True)
-        gram_copy = move(2 * s + 1, gram_out.at[s], gram_in.at[s], 1)
-        next_uu = half[:BLOCK, :BLOCK] + dot3(turn[:, :BLOCK], half[:, :BLOCK], True)
-        upper = pair[:, :BLOCK] + dot3(pair, turn[:, :BLOCK])
-        return turn[:, :BLOCK], upper, next_uu, turn_copy, gram_copy
-
-    def cross_gram(s, left_turn, cross):
-        right_turn = turn_in[s]
-        half = cross[:, BLOCK:] + dot3(cross, right_turn)
+        return (half[:BLOCK, :BLOCK] + dot3(turn[:, :BLOCK], half[:, :BLOCK], True),
+                half[BLOCK:, BLOCK:] + dot3(turn[:, BLOCK:], half[:, BLOCK:], True))
+
+    def cross_gram(left_turn, right_turn, cross):
+        half = cross[1] + (dot3(cross[0], right_turn[:BLOCK]) + dot3(cross[1], right_turn[BLOCK:]))
         return half[:BLOCK] + dot3(left_turn, half, True)
 
     load.wait()
     pair = x_ref[...]
     local = dot3(pair, pair, True)
     payload = jnp.concatenate([local[:BLOCK, BLOCK:], local[:BLOCK, :BLOCK], local[BLOCK:, BLOCK:]], axis=0)
-    pl.semaphore_wait(barrier, (n_near - 1) + (n_far - 1) + (n_wide - 1))
+    pl.semaphore_wait(barrier, 3 * (n_near - 1) + (n_far - 1) + (n_wide - 1))
+    next_up = move(4, x_ref.at[:, :BLOCK], next_x.at[0], 1)
+    next_low = move(10, x_ref.at[:, BLOCK:], next_x.at[1], 1)
     grams = scatter(0, payload)
-    next_copy = move(4, x_ref, next_x, 1)
     grams = across(0, grams)
-    next_copy.wait_recv()
-    next_pair = next_x[...]
-    crosses = scatter(1, blocks(dot3(pair, next_pair, True)))
+    next_up.wait_recv()
+    crosses_up = scatter(1, dot3(pair, next_x[0], True))
+    next_low.wait_recv()
+    crosses_low = scatter(2, dot3(pair, next_x[1], True))
+    next_pair = jnp.concatenate([next_x[0], next_x[1]], axis=1)
+    crosses_up = across(1, crosses_up)
     grams = gather(0, grams)
-    crosses = across(1, crosses)
+    crosses_low = across(2, crosses_low)
+    crosses_up = gather(1, crosses_up)
     gram = reduced(0, grams)
-    left_turn, upper, uu, turn_copy, gram_copy = first_round(
-        0, pair, gram[BLOCK:2 * BLOCK], gram[:BLOCK], gram[2 * BLOCK:])
-    crosses = gather(1, crosses)
+    ul, uu, ll = gram[:BLOCK], gram[BLOCK:2 * BLOCK], gram[2 * BLOCK:]
+    turn = turn_of(uu, ul, ll)
+    turn_out[...] = turn[:, BLOCK:]
+    turn_copy = move(0, turn_out, turn_in, 1)
+    crosses_low = gather(2, crosses_low)
+    uu, gram_out[...] = turned(turn, uu, ul, ll)
+    gram_copy = move(1, gram_out, gram_in, 1)
+    left_turn = turn[:, :BLOCK]
+    upper = pair[:, :BLOCK] + dot3(pair, left_turn)
     turn_copy.wait_recv()
-    right_turn = turn_in[0]
+    right_turn = turn_in[...]
     lower = next_pair[:, BLOCK:] + dot3(next_pair, right_turn)
     pair = jnp.concatenate([upper, lower], axis=1)
     gram_copy.wait_recv()
-    cross = reduced(1, crosses)
-    cross = joined(cross[:BLOCK], cross[BLOCK:2 * BLOCK], cross[2 * BLOCK:3 * BLOCK], cross[3 * BLOCK:])
-    ul, ll = cross_gram(0, left_turn, cross), gram_in[0]
+    cross = reduced(1, crosses_up), reduced(2, crosses_low)
+    ul, ll = cross_gram(left_turn, right_turn, cross), gram_in[...]
     turn = turn_of(uu, ul, ll)
     up_out[...] = pair[:, :BLOCK] + dot3(pair, turn[:, :BLOCK])
     up_copy = move(5, up_out, up_in, -1)
     low_out[...] = pair[:, BLOCK:] + dot3(pair, turn[:, BLOCK:])
     low_copy = move(6, low_out, low_in, 1)
-    full = joined(uu, ul, ul.T, ll)
-    half = full + dot3(full, turn)
-    upgram_out[...] = half[:BLOCK, :BLOCK] + dot3(turn[:, :BLOCK], half[:, :BLOCK], True)
+    upgram_out[...], lowgram_out[...] = turned(turn, uu, ul, ll)
     upgram_copy = move(7, upgram_out, upgram_in, -1)
-    ll = half[BLOCK:, BLOCK:] + dot3(turn[:, BLOCK:], half[:, BLOCK:], True)
+    lowgram_copy = move(2, lowgram_out, lowgram_in, 1)
 
     kept_up, kept_low = up_out[...], low_out[...]
     low_up = dot3(kept_low, kept_up, True)
     up_copy.wait_recv()
     upper = up_in[...]
-    grams = scatter(2, dot3(kept_low, upper, True))
-    up_up = dot3(upper, kept_up, True)
+    grams = scatter(3, dot3(kept_low, upper, True))
+    crosses_up = scatter(4, jnp.concatenate([dot3(upper, kept_up, True), low_up], axis=0))
+    pair = jnp.concatenate([upper, kept_low], axis=1)
     low_copy.wait_recv()
     next_low = low_in[...]
+    crosses_low = scatter(5, dot3(pair, next_low, True))
     next_pair = jnp.concatenate([kept_up, next_low], axis=1)
-    pair = jnp.concatenate([upper, kept_low], axis=1)
-    right = dot3(pair, next_low, True)
-    crosses = scatter(3, jnp.concatenate([up_up, right[:BLOCK], low_up, right[BLOCK:]], axis=0))
-    grams = across(2, grams)
-    crosses = across(3, crosses)
-    grams = gather(2, grams)
+    grams = across(3, grams)
+    crosses_up = across(4, crosses_up)
+    crosses_low = across(5, crosses_low)
+    grams = gather(3, grams)
+    next_grams = [
+        send(reduces[3][3].at[me_near], next_whole.at[me_near], next_send.at[k], next_recv.at[k], next_near(k, 1))
+        for k in range(n_near)
+    ]
+    crosses_up = gather(4, crosses_up)
+    crosses_low = gather(5, crosses_low)
     upgram_copy.wait_recv()
-    ul = reduced(2, grams).T
-    left_turn, upper, uu, turn_copy, gram_copy = first_round(1, pair, upgram_in[...], ul, ll)
-    crosses = gather(3, crosses)
-    turn_copy.wait_recv()
-    right_turn = turn_in[1]
+    uu, ul, ll = upgram_in[...], reduced(3, grams).T, lowgram_out[...]
+    turn = turn_of(uu, ul, ll)
+    left_turn = turn[:, :BLOCK]
+    lowgram_copy.wait_recv()
+    arrived(next_grams)
+    next_uu, next_ul, next_ll = upgram_out[...], next_whole[...].reshape(BLOCK, BLOCK).T, lowgram_in[...]
+    next_turn = turn_of(next_uu, next_ul, next_ll)
+    right_turn = next_turn[:, BLOCK:]
+    upper = pair[:, :BLOCK] + dot3(pair, left_turn)
     lower = next_pair[:, BLOCK:] + dot3(next_pair, right_turn)
     pair = jnp.concatenate([upper, lower], axis=1)
-    gram_copy.wait_recv()
-    cross = reduced(3, crosses)
-    cross = joined(cross[:BLOCK], cross[BLOCK:2 * BLOCK], cross[2 * BLOCK:3 * BLOCK], cross[3 * BLOCK:])
-    turn = turn_of(uu, cross_gram(1, left_turn, cross), gram_in[1])
+    uu, _ = turned(turn, uu, ul, ll)
+    _, ll = turned(next_turn, next_uu, next_ul, next_ll)
+    cross = reduced(4, crosses_up), reduced(5, crosses_low)
+    turn = turn_of(uu, cross_gram(left_turn, right_turn, cross), ll)
+    if series:
+        flag_out[...] = jnp.broadcast_to(worst, flag_out.shape)
+        flags[wide] = flag_out[...]
+        marks = [
+            send(flag_out, flags.at[wide], flag_send.at[k], flag_recv.at[k], wide_peer(k)) for k in range(1, n_wide)
+        ]
     last_low_out[...] = pair[:, BLOCK:] + dot3(pair, turn[:, BLOCK:])
     last_low = move(8, last_low_out, last_low_in, -2)
     last_up_out[...] = pair[:, :BLOCK] + dot3(pair, turn[:, :BLOCK])
     last_up = move(9, last_up_out, last_up_in, 1)
 
     if series:
-        flag_out[...] = jnp.broadcast_to(worst, flag_out.shape)
-        flags[wide] = flag_out[...]
-        arrived([
-            send(flag_out, flags.at[wide], flag_send.at[k], flag_recv.at[k], wide_peer(k)) for k in range(1, n_wide)
-        ])
+        arrived(marks)
         flag_ref[0, 0] = jnp.max(jnp.where(flags[...] <= SERIES_TOL, 0, 1))
     else:
         flag_ref[0, 0] = 0
@@ -307,17 +323,18 @@
     sems = pltpu.SemaphoreType.DMA
     peers = max(n_near, n_far)
     scratch = [vmem(rows, width)]
-    for count in (3, 4, 1, 4):
+    for count in (3, 2, 2, 1, 2, 2):
         piece = count * BLOCK // n_near
         scratch += [vmem(n, piece, BLOCK) for n in (n_near, n_near, n_far, n_near)]
     scratch += [
-        vmem(rows, width),
-        vmem(2, width, BLOCK), vmem(2, width, BLOCK), vmem(2, BLOCK, BLOCK), vmem(2, BLOCK, BLOCK),
+        vmem(2, rows, BLOCK),
+        vmem(width, BLOCK), vmem(width, BLOCK), vmem(BLOCK, BLOCK), vmem(BLOCK, BLOCK),
+        vmem(BLOCK, BLOCK), vmem(BLOCK, BLOCK), vmem(n_near, BLOCK // n_near, BLOCK),
         vmem(rows, BLOCK), vmem(rows, BLOCK), vmem(BLOCK, BLOCK), vmem(BLOCK, BLOCK),
         vmem(rows, BLOCK), vmem(rows, BLOCK),
         vmem(rows, BLOCK), vmem(rows, BLOCK), vmem(rows, BLOCK), vmem(rows, BLOCK),
         vmem(8, BLOCK), vmem(n_wide, 8, BLOCK), vmem(2, width, width),
-        sems((4, 3, peers)), sems((4, 3, peers)), sems((10,)), sems((10,)), sems((n_wide,)), sems((n_wide,)), sems,
+        sems((6, 3, peers)), sems((6, 3, peers)), sems((11,)), sems((11,)), sems((n_wide,)), sems((n_wide,)), sems((n_near,)), sems((n_near,)), sems,
     ]
     return pl.pallas_call(
         functools.partial(kernel, n_wide, n_near, n_far, series),

time: 227 us -> 237 us (1.044)
  Pallas kernels: 225 us -> 235 us
    pallas_call x2, Pallas kernels: 225 us -> 235 us  [run(): pl.pallas_call(functools.partial(kernel, n_wide, n_near, n_far, series),...]
where the time goes in v4:
time: 237 us
  Pallas kernels  235 us (99%)
    pallas_call x2, Pallas kernels, run(): pl.pallas_call(functools.partial(kernel, n_wide, n_near, n_far, series),...  235 us

profile of v4, /device:TPU:1, one launch (start us, length us, event | category | flops | bytes accessed | tf_op | source)
XLA Modules:
  0.0 236.6 jit_solution(8805824127819463825)
XLA Ops:
  0.0 0.0 copy-start
  0.0 75.6 %jacobi_series.1 = (f32[256,256]{1,0:T(8,128)S(1)}, s32[1,1]{1,0:T(1,128)}) custom-call(f32[256,256]{1,0:T(8,128)} %x_hbm.2), custom_call_target="tpu_custom_call" | custom-call | tf_op jit(solution)/shard_map/jacobi_series/pallas_call | solution.py:339
  76.2 0.0 copy-done
  76.2 159.6 %conditional.1 = (f32[256,256]{1,0:T(8,128)S(1)}) conditional(s32[]{:T(128)} %bitcast, f32[256,256]{1,0:T(8,128)S(1)} %get-tuple-element.14, f32[256,256]{1,0:T(8,128)S(1)} %copy-done), branch_computations={%region_0.0_spmd, %region_1.0_spmd} | conditional | bytes 8 | solution.py:355
  76.4 159.2 %jacobi_newton.1 = (f32[256,256]{1,0:T(8,128)S(1)}, s32[1,1]{1,0:T(1,128)}) custom-call(f32[256,256]{1,0:T(8,128)S(1)} %x_hbm.1), custom_call_target="tpu_custom_call" | custom-call | tf_op jit(solution)/shard_map/cond/branch_1_fun/jacobi_newton/pallas_call | solution.py:339
  235.8 0.7 copy.7
Async XLA Ops:
  0.0 76.2 %copy-start = (f32[256,256]{1,0:T(8,128)S(1)}, f32[256,256]{1,0:T(8,128)}, u32[]{:S(2)}) copy-start(f32[256,256]{1,0:T(8,128)} %x_hbm.2) | copy-start | bytes 786436

commit v5 on v4

--- a/solution.py
+++ b/solution.py
@@ -37,6 +37,10 @@
 
 def dot6(a, b):
     return lax.dot_general(a, b, dims(False, False), precision=lax.Precision.HIGHEST, preferred_element_type=F32)
+
+
+def far_first(count):
+    return sorted(range(1, count), key=lambda k: abs(2 * k - count))
 
 
 def iotas(shape):
@@ -154,7 +158,7 @@
         out, near, far, whole = reduces[i]
         out[...] = payload.reshape(out.shape)
         copies = []
-        for k in range(1, n_near):
+        for k in far_first(n_near):
             other, peer = near_peer(k)
             copies.append(
                 send(out.at[other], near.at[me_near], reduce_send.at[i, 0, k], reduce_recv.at[i, 0, k], peer))
@@ -177,7 +181,7 @@
         return [
             send(whole.at[me_near], whole.at[me_near], reduce_send.at[i, 2, k], reduce_recv.at[i, 2, k],
                  near_peer(k)[1])
-            for k in range(1, n_near)
+            for k in far_first(n_near)
         ]
 
     def reduced(i, copies):
@@ -298,8 +302,11 @@
         marks = [
             send(flag_out, flags.at[wide], flag_send.at[k], flag_recv.at[k], wide_peer(k)) for k in range(1, n_wide)
         ]
-    last_low_out[...] = pair[:, BLOCK:] + dot3(pair, turn[:, BLOCK:])
-    last_low = move(8, last_low_out, last_low_in, -2)
+    half = pair.shape[0] // 2
+    last_low_out[:half] = pair[:half, BLOCK:] + dot3(pair[:half], turn[:, BLOCK:])
+    last_low = move(8, last_low_out.at[:half], last_low_in.at[:half], -2)
+    last_low_out[half:] = pair[half:, BLOCK:] + dot3(pair[half:], turn[:, BLOCK:])
+    last_low2 = move(3, last_low_out.at[half:], last_low_in.at[half:], -2)
     last_up_out[...] = pair[:, :BLOCK] + dot3(pair, turn[:, :BLOCK])
     last_up = move(9, last_up_out, last_up_in, 1)
 
@@ -311,6 +318,7 @@
     last_up.wait_recv()
     out_ref[:, :BLOCK] = last_up_in[...]
     last_low.wait_recv()
+    last_low2.wait_recv()
     out_ref[:, BLOCK:] = last_low_in[...]
     for copy in sends:
         copy.wait_send()

time: 237 us -> 236 us (level)
  no operation moved by 1% of the time
where the time goes in v5:
time: 236 us
  Pallas kernels  234 us (99%)
    pallas_call x2, Pallas kernels, run(): pl.pallas_call(functools.partial(kernel, n_wide, n_near, n_far, series),...  234 us

profile of v5, /device:TPU:1, one launch (start us, length us, event | category | flops | bytes accessed | tf_op | source)
XLA Modules:
  0.0 235.7 jit_solution(10641496314768887948)
XLA Ops:
  0.0 0.0 copy-start
  0.0 74.6 %jacobi_series.1 = (f32[256,256]{1,0:T(8,128)S(1)}, s32[1,1]{1,0:T(1,128)}) custom-call(f32[256,256]{1,0:T(8,128)} %x_hbm.2), custom_call_target="tpu_custom_call" | custom-call | tf_op jit(solution)/shard_map/jacobi_series/pallas_call | solution.py:347
  75.2 0.0 copy-done
  75.2 159.8 %conditional.1 = (f32[256,256]{1,0:T(8,128)S(1)}) conditional(s32[]{:T(128)} %bitcast, f32[256,256]{1,0:T(8,128)S(1)} %get-tuple-element.14, f32[256,256]{1,0:T(8,128)S(1)} %copy-done), branch_computations={%region_0.0_spmd, %region_1.0_spmd} | conditional | bytes 8 | solution.py:363
  75.4 159.4 %jacobi_newton.1 = (f32[256,256]{1,0:T(8,128)S(1)}, s32[1,1]{1,0:T(1,128)}) custom-call(f32[256,256]{1,0:T(8,128)S(1)} %x_hbm.1), custom_call_target="tpu_custom_call" | custom-call | tf_op jit(solution)/shard_map/cond/branch_1_fun/jacobi_newton/pallas_call | solution.py:347
  235.0 0.7 copy.7
Async XLA Ops:
  0.0 75.2 %copy-start = (f32[256,256]{1,0:T(8,128)S(1)}, f32[256,256]{1,0:T(8,128)}, u32[]{:S(2)}) copy-start(f32[256,256]{1,0:T(8,128)} %x_hbm.2) | copy-start | bytes 786436

commit v6 on v5

--- a/solution.py
+++ b/solution.py
@@ -99,9 +99,9 @@
 
 def kernel(n_wide, n_near, n_far, series, x_hbm, out_ref, flag_ref, x_ref, *refs):
     (reduces, (next_x, turn_out, turn_in, gram_out, gram_in, lowgram_out, lowgram_in, next_whole, up_out, up_in, upgram_out, upgram_in, low_out, low_in,
-               last_low_out, last_low_in, last_up_out, last_up_in, flag_out, flags, newton),
+               last_low_out, last_up_out, flag_out, flags, newton),
      (reduce_send, reduce_recv, move_send, move_recv, flag_send, flag_recv, next_send, next_recv, load_sem)) = (
-        [refs[4 * i:4 * i + 4] for i in range(6)], refs[24:45], refs[45:])
+        [refs[4 * i:4 * i + 4] for i in range(6)], refs[24:43], refs[43:])
     wide, row = lax.axis_index("wide"), lax.axis_index("row")
     me_near, me_far = lax.rem(row, n_near), lax.div(row, n_near)
 
@@ -255,9 +255,6 @@
     up_copy = move(5, up_out, up_in, -1)
     low_out[...] = pair[:, BLOCK:] + dot3(pair, turn[:, BLOCK:])
     low_copy = move(6, low_out, low_in, 1)
-    upgram_out[...], lowgram_out[...] = turned(turn, uu, ul, ll)
-    upgram_copy = move(7, upgram_out, upgram_in, -1)
-    lowgram_copy = move(2, lowgram_out, lowgram_in, 1)
 
     kept_up, kept_low = up_out[...], low_out[...]
     low_up = dot3(kept_low, kept_up, True)
@@ -269,6 +266,9 @@
     low_copy.wait_recv()
     next_low = low_in[...]
     crosses_low = scatter(5, dot3(pair, next_low, True))
+    upgram_out[...], lowgram_out[...] = turned(turn, uu, ul, ll)
+    upgram_copy = move(7, upgram_out, upgram_in, -1)
+    lowgram_copy = move(2, lowgram_out, lowgram_in, 1)
     next_pair = jnp.concatenate([kept_up, next_low], axis=1)
     grams = across(3, grams)
     crosses_up = across(4, crosses_up)
@@ -304,11 +304,11 @@
         ]
     half = pair.shape[0] // 2
     last_low_out[:half] = pair[:half, BLOCK:] + dot3(pair[:half], turn[:, BLOCK:])
-    last_low = move(8, last_low_out.at[:half], last_low_in.at[:half], -2)
+    last_low = move(8, last_low_out.at[:half], out_ref.at[:half, BLOCK:], -2)
     last_low_out[half:] = pair[half:, BLOCK:] + dot3(pair[half:], turn[:, BLOCK:])
-    last_low2 = move(3, last_low_out.at[half:], last_low_in.at[half:], -2)
+    last_low2 = move(3, last_low_out.at[half:], out_ref.at[half:, BLOCK:], -2)
     last_up_out[...] = pair[:, :BLOCK] + dot3(pair, turn[:, :BLOCK])
-    last_up = move(9, last_up_out, last_up_in, 1)
+    last_up = move(9, last_up_out, out_ref.at[:, :BLOCK], 1)
 
     if series:
         arrived(marks)
@@ -316,10 +316,8 @@
     else:
         flag_ref[0, 0] = 0
     last_up.wait_recv()
-    out_ref[:, :BLOCK] = last_up_in[...]
     last_low.wait_recv()
     last_low2.wait_recv()
-    out_ref[:, BLOCK:] = last_low_in[...]
     for copy in sends:
         copy.wait_send()
 
@@ -340,7 +338,7 @@
         vmem(BLOCK, BLOCK), vmem(BLOCK, BLOCK), vmem(n_near, BLOCK // n_near, BLOCK),
         vmem(rows, BLOCK), vmem(rows, BLOCK), vmem(BLOCK, BLOCK), vmem(BLOCK, BLOCK),
         vmem(rows, BLOCK), vmem(rows, BLOCK),
-        vmem(rows, BLOCK), vmem(rows, BLOCK), vmem(rows, BLOCK), vmem(rows, BLOCK),
+        vmem(rows, BLOCK), vmem(rows, BLOCK),
         vmem(8, BLOCK), vmem(n_wide, 8, BLOCK), vmem(2, width, width),
         sems((6, 3, peers)), sems((6, 3, peers)), sems((11,)), sems((11,)), sems((n_wide,)), sems((n_wide,)), sems((n_near,)), sems((n_near,)), sems,
     ]

time: 236 us -> 236 us (level)
  no operation moved by 1% of the time
where the time goes in v6:
time: 236 us; the launch traced here: 234 us
  Pallas kernels  232 us (98%)
    pallas_call x2, Pallas kernels, run(): pl.pallas_call(functools.partial(kernel, n_wide, n_near, n_far, series),...  232 us

profile of v6, /device:TPU:1, one launch (start us, length us, event | category | flops | bytes accessed | tf_op | source)
XLA Modules:
  0.0 234.0 jit_solution(1506572182545496471)
XLA Ops:
  0.0 0.0 copy-start
  0.0 74.2 %jacobi_series.1 = (f32[256,256]{1,0:T(8,128)S(1)}, s32[1,1]{1,0:T(1,128)}) custom-call(f32[256,256]{1,0:T(8,128)} %x_hbm.2), custom_call_target="tpu_custom_call" | custom-call | tf_op jit(solution)/shard_map/jacobi_series/pallas_call | solution.py:345
  74.8 0.0 copy-done
  74.8 158.4 %conditional.1 = (f32[256,256]{1,0:T(8,128)S(1)}) conditional(s32[]{:T(128)} %bitcast, f32[256,256]{1,0:T(8,128)S(1)} %get-tuple-element.14, f32[256,256]{1,0:T(8,128)S(1)} %copy-done), branch_computations={%region_0.0_spmd, %region_1.0_spmd} | conditional | bytes 8 | solution.py:361
  75.0 158.0 %jacobi_newton.1 = (f32[256,256]{1,0:T(8,128)S(1)}, s32[1,1]{1,0:T(1,128)}) custom-call(f32[256,256]{1,0:T(8,128)S(1)} %x_hbm.1), custom_call_target="tpu_custom_call" | custom-call | tf_op jit(solution)/shard_map/cond/branch_1_fun/jacobi_newton/pallas_call | solution.py:345
  233.3 0.7 copy.7
Async XLA Ops:
  0.0 74.8 %copy-start = (f32[256,256]{1,0:T(8,128)S(1)}, f32[256,256]{1,0:T(8,128)}, u32[]{:S(2)}) copy-start(f32[256,256]{1,0:T(8,128)} %x_hbm.2) | copy-start | bytes 786436
